TPU v7x, 32 devices: a whole 2x2x4 slice. The times are simulated.
32 devices in a mesh: seq: 8 (over z, y), tp: 4 (over x, core).
Axes of the slice: x: 2, y: 2, z: 4, core: 2. Of those that a mesh axis runs over, the one named last changes fastest.
Arguments:
- tokens: bfloat16 [8192, 1152], P('seq', 'tp'), may hold values from -6 to 6
- out_grad: bfloat16 [8192, 1152], P('seq', 'tp'), may hold values from -6 to 6
- route_mask: int32 [8192], P('seq'), may hold values from 0 to 1, as said below
- kept_counts: int32 [32], replicated, may hold values from 64 to 192, as said below
- labels: int32 [32], replicated, may hold values from 0 to 1000
- timesteps: int32 [32], replicated, may hold values from 0 to 999
- class_table: bfloat16 [1001, 1152], replicated, may hold values from -6 to 6
- ada_weight: bfloat16 [1152, 6, 1152], P(None, None, 'tp'), may hold values from -0.1875 to 0.1875
- ada_bias: bfloat16 [6, 1152], P(None, 'tp'), may hold values from -2 to 2
- qkv_weight: bfloat16 [1152, 3, 1152], P(None, None, 'tp'), may hold values from -0.1875 to 0.1875
- qv_bias: bfloat16 [2, 1152], P(None, 'tp'), may hold values from -2 to 2
- proj_weight: bfloat16 [1152, 1152], P('tp'), may hold values from -0.5 to 0.5
- proj_bias: bfloat16 [1152], P('tp'), may hold values from -2 to 2
- hidden_weight: bfloat16 [1152, 4608], P(None, 'tp'), may hold values from -0.1875 to 0.1875
- hidden_bias: bfloat16 [4608], P('tp'), may hold values from -2 to 2
- output_weight: bfloat16 [4608, 1152], P('tp'), may hold values from -0.09375 to 0.09375
- output_bias: bfloat16 [1152], P('tp'), may hold values from -2 to 2
Outputs:
- output: bfloat16 [8192, 1152], P('seq', 'tp')
- tokens_grad: bfloat16 [8192, 1152], P('seq', 'tp')
- class_grad: float32 [1001, 1152], P(None, 'seq')
- ada_weight_grad: float32 [1152, 6, 1152], P('seq', None, 'tp')
- ada_bias_grad: float32 [6, 1152], P(None, 'tp')
- qkv_weight_grad: float32 [1152, 3, 1152], P('seq', None, 'tp')
- qv_bias_grad: float32 [2, 1152], P(None, 'tp')
- proj_weight_grad: float32 [1152, 1152], P('tp', 'seq')
- proj_bias_grad: float32 [1152], P('tp')
- hidden_weight_grad: float32 [1152, 4608], P('seq', 'tp')
- hidden_bias_grad: float32 [4608], P('tp')
- output_weight_grad: float32 [4608, 1152], P('tp', 'seq')
- output_bias_grad: float32 [1152], P('tp')
Inputs may be any that keep to these rules, and one draw needn't show every extreme that they name: route_mask keeps exactly kept_counts[i] of the 256 tokens of image i. The kept tokens of all images number 512 * 8; the kept tokens of the first j * 4 images exceed j * 512 by 0 to 128 for every j, by exactly 128 for some j, and by 0 at the end. Every aligned block of 4 images has one image with 192 kept tokens. `route_mask`: consistent with kept_counts.
All inputs are finite; a program needn't handle non-finite values.
Results may differ from a plain program's by a relative error of at most 0.025.
The roundings to bfloat16 on the way count: a program that leaves them out, or rounds other values in their place, can miss the bound.
Values may be sent and summed in bfloat16 or wider, within the bound.
A program may use at most 192 MiB of HBM per device.

v0:
```python
import math
import jax
import jax.numpy as jnp
from jax import lax
from jax.sharding import PartitionSpec as P

HEAD_DIM = 72
IMG_DEV = 4
ROWS = 640
NORM_EPS = 1e-06
HIGHEST = lax.Precision.HIGHEST


def exact_dot(left_mat, right_mat):
    return jnp.dot(left_mat, right_mat, precision=HIGHEST, preferred_element_type=jnp.float32)


def time_embed(step_ids, model_width):
    half_width = model_width // 2
    frequency = jnp.exp(-math.log(10000.0) * jnp.arange(half_width, dtype=jnp.float32) / half_width)
    angles = step_ids.astype(jnp.float32)[:, None] * frequency[None, :]
    return jnp.concatenate([jnp.cos(angles), jnp.sin(angles)], axis=1)


def norm_rows(values):
    centered = values - jnp.mean(values, axis=1, keepdims=True)
    inverse = lax.rsqrt(jnp.mean(centered * centered, axis=1, keepdims=True) + NORM_EPS)
    return (centered * inverse, inverse)


def gelu_tanh(values):
    return jax.nn.gelu(values, approximate=True)


def local(
    tokens,
    out_grad,
    route_mask,
    kept_counts,
    labels,
    timesteps,
    class_table,
    ada_weight,
    ada_bias,
    qkv_weight,
    qv_bias,
    proj_weight,
    proj_bias,
    hidden_weight,
    hidden_bias,
    output_weight,
    output_bias,
):
    f32, bf16 = (jnp.float32, jnp.bfloat16)
    seq_index = lax.axis_index("seq")
    tp_index = lax.axis_index("tp")
    seq_size = lax.axis_size("seq")
    col_local = tokens.shape[1]
    model_width = class_table.shape[1]
    head_cols = qkv_weight.shape[2]
    heads_local = head_cols // HEAD_DIM
    slice_width = model_width // seq_size
    images = kept_counts.shape[0]
    scale_factor = HEAD_DIM ** (-0.5)
    col_start = tp_index * col_local
    first_image = seq_index * IMG_DEV
    own_counts = lax.dynamic_slice_in_dim(kept_counts, first_image, IMG_DEV)
    own_ends = jnp.cumsum(own_counts)
    rank = jnp.where(route_mask > 0, jnp.cumsum(route_mask) - 1, -1)
    row_ids = jnp.arange(ROWS, dtype=jnp.int32)
    place = (rank[None, :] == row_ids[:, None]).astype(bf16)
    row_image = jnp.sum((own_ends[None, :] <= row_ids[:, None]).astype(jnp.int32), axis=1)
    row_onehot = (row_image[:, None] == jnp.arange(IMG_DEV, dtype=jnp.int32)[None, :]).astype(f32)

    def whole_rows(part_rows):
        return lax.all_gather(part_rows, "tp", axis=1, tiled=True)

    def column_sum(part_rows):
        return lax.psum_scatter(
            part_rows.astype(bf16), "tp", scatter_dimension=1, tiled=True
        ).astype(f32)

    def own_cols(full_rows):
        return lax.dynamic_slice_in_dim(full_rows, col_start, col_local, 1)

    def reinsert(rows_new, initial):
        placed = jnp.einsum("rt,rc->tc", place, rows_new, preferred_element_type=f32).astype(bf16)
        return jnp.where(route_mask[:, None] > 0, placed, initial)

    label_hot = (
        labels[:, None] == jnp.arange(class_table.shape[0], dtype=jnp.int32)[None, :]
    ).astype(bf16)
    condition = jnp.dot(label_hot, class_table, preferred_element_type=f32) + time_embed(
        timesteps, model_width
    )
    cond_low = jax.nn.silu(condition).astype(bf16)
    cond_own = lax.dynamic_slice_in_dim(cond_low, first_image, IMG_DEV)
    mod_own = (
        jnp.einsum("wd,dcf->wcf", cond_own, ada_weight, preferred_element_type=f32)
        + ada_bias.astype(f32)[None]
    )
    mod_full = lax.all_gather(mod_own, "tp", axis=2, tiled=True)

    def row_full(stretch_id):
        return exact_dot(row_onehot, mod_full[:, stretch_id, :])

    def row_own(stretch_id):
        return exact_dot(row_onehot, mod_own[:, stretch_id, :])

    def input_grads(partial_rows, normed, inverse, scale):
        own_grad = column_sum(partial_rows)
        normed_own = own_cols(normed)
        scaled_grad = own_grad * (1.0 + own_cols(scale))
        mean_grad, mean_cross = lax.psum(
            (
                jnp.sum(scaled_grad, axis=1, keepdims=True) / model_width,
                jnp.sum(scaled_grad * normed_own, axis=1, keepdims=True) / model_width,
            ),
            "tp",
        )
        return (
            own_grad,
            own_grad * normed_own,
            inverse * (scaled_grad - mean_grad - normed_own * mean_cross),
        )

    picked = jnp.dot(place, jnp.concatenate([tokens, out_grad], axis=1), preferred_element_type=f32)
    rows_in = picked[:, :col_local].astype(bf16)
    grad_rows = picked[:, col_local:]
    gate_one = row_own(2)
    gate_two = row_own(5)
    mlp_grad = (grad_rows * gate_two).astype(bf16)
    full_in = whole_rows(rows_in).astype(f32)
    mlp_grad_full = whole_rows(mlp_grad)
    normed_one, inverse_one = norm_rows(full_in)
    scale_one = row_full(1)
    branch_one = (normed_one * (1.0 + scale_one) + row_full(0)).astype(bf16)
    qkv_bias = jnp.stack([qv_bias[0], jnp.zeros_like(qv_bias[0]), qv_bias[1]]).astype(f32)
    qkv_rows = (
        jnp.einsum("rd,dcf->rcf", branch_one, qkv_weight, preferred_element_type=f32)
        + qkv_bias[None]
    ).astype(bf16)
    query_all, key_all, value_all = (
        qkv_rows[:, part].reshape(ROWS, heads_local, HEAD_DIM) for part in range(3)
    )
    same_image = row_image[:, None] == row_image[None, :]
    raw = jnp.einsum("qhe,khe->hqk", query_all, key_all, preferred_element_type=f32) * scale_factor
    masked = jnp.where(same_image[None], raw, -1e30)
    top_score = jnp.max(masked, axis=2, keepdims=True)
    exp_scores = jnp.exp(masked - top_score)
    attn_probs = exp_scores / jnp.sum(exp_scores, axis=2, keepdims=True)
    probs_low = attn_probs.astype(bf16)
    attended = (
        jnp.einsum("hqk,khe->qhe", probs_low, value_all, preferred_element_type=f32)
        .reshape(ROWS, head_cols)
        .astype(bf16)
    )
    attn_out = column_sum(
        jnp.dot(attended, proj_weight, preferred_element_type=f32)
    ) + proj_bias.astype(f32)
    middle = rows_in.astype(f32) + gate_one * attn_out
    middle_full = whole_rows(middle.astype(bf16)).astype(f32)
    normed_two, inverse_two = norm_rows(middle_full)
    scale_two = row_full(4)
    branch_two = (normed_two * (1.0 + scale_two) + row_full(3)).astype(bf16)
    pre_act = jnp.dot(branch_two, hidden_weight, preferred_element_type=f32) + hidden_bias.astype(
        f32
    )
    act_low = gelu_tanh(pre_act).astype(bf16)
    mlp_out = column_sum(
        jnp.dot(act_low, output_weight, preferred_element_type=f32)
    ) + output_bias.astype(f32)
    final_rows = middle + gate_two * mlp_out
    output = reinsert(final_rows.astype(bf16), tokens)
    gate_two_rows = grad_rows * mlp_out
    output_bias_term = jnp.sum(mlp_grad, axis=0, dtype=f32)
    output_weight_term = jnp.einsum(
        "rf,rd->fd", act_low, mlp_grad_full, preferred_element_type=f32
    ).astype(bf16)
    act_grad = jnp.einsum("rd,fd->rf", mlp_grad_full, output_weight, preferred_element_type=f32)
    gelu_pull = jax.vjp(gelu_tanh, pre_act)[1]
    pre_grad = gelu_pull(act_grad)[0].astype(bf16)
    hidden_bias_term = jnp.sum(pre_grad, axis=0, dtype=f32)
    hidden_weight_term = jnp.einsum(
        "rd,rf->df", branch_two, pre_grad, preferred_element_type=f32
    ).astype(bf16)
    two_partial = jnp.einsum("rf,df->rd", pre_grad, hidden_weight, preferred_element_type=f32)
    shift_two_grad, scale_two_grad, two_norm_grad = input_grads(
        two_partial, normed_two, inverse_two, scale_two
    )
    middle_grad = grad_rows + two_norm_grad
    gate_one_rows = middle_grad * attn_out
    attn_grad = (middle_grad * gate_one).astype(bf16)
    proj_bias_term = jnp.sum(attn_grad, axis=0, dtype=f32)
    attn_grad_full = whole_rows(attn_grad)
    proj_weight_term = jnp.einsum(
        "rf,rd->fd", attended, attn_grad_full, preferred_element_type=f32
    ).astype(bf16)
    attended_grad = (
        jnp.einsum("rd,fd->rf", attn_grad_full, proj_weight, preferred_element_type=f32)
        .astype(bf16)
        .reshape(ROWS, heads_local, HEAD_DIM)
    )
    value_term = jnp.einsum("hqk,qhe->khe", probs_low, attended_grad, preferred_element_type=f32)
    prob_grad = jnp.einsum("qhe,khe->hqk", attended_grad, value_all, preferred_element_type=f32)
    row_dot = jnp.sum(attn_probs * prob_grad, axis=2, keepdims=True)
    score_grad = (attn_probs * (prob_grad - row_dot)).astype(bf16)
    query_term = (
        jnp.einsum("hqk,khe->qhe", score_grad, key_all, preferred_element_type=f32) * scale_factor
    )
    key_term = (
        jnp.einsum("hqk,qhe->khe", score_grad, query_all, preferred_element_type=f32) * scale_factor
    )
    qkv_grad = (
        jnp.stack([query_term, key_term, value_term], axis=1)
        .reshape(ROWS, 3, head_cols)
        .astype(bf16)
    )
    qkv_sums = jnp.sum(qkv_grad, axis=0, dtype=f32)
    qkv_weight_term = jnp.einsum(
        "rd,rcf->dcf", branch_one, qkv_grad, preferred_element_type=f32
    ).astype(bf16)
    one_partial = jnp.einsum("rcf,dcf->rd", qkv_grad, qkv_weight, preferred_element_type=f32)
    shift_one_grad, scale_one_grad, one_norm_grad = input_grads(
        one_partial, normed_one, inverse_one, scale_one
    )
    in_grad = middle_grad + one_norm_grad
    tokens_grad = reinsert(in_grad.astype(bf16), out_grad)
    per_row = jnp.concatenate(
        [
            shift_one_grad,
            scale_one_grad,
            gate_one_rows,
            shift_two_grad,
            scale_two_grad,
            gate_two_rows,
        ],
        axis=1,
    )
    mod_grad = jnp.einsum(
        "rw,rf->wf", row_onehot, per_row, precision=HIGHEST, preferred_element_type=f32
    )
    small = jnp.concatenate(
        [
            mod_grad.reshape(-1),
            qkv_sums[0],
            qkv_sums[2],
            proj_bias_term,
            hidden_bias_term,
            output_bias_term,
        ]
    )
    small_all = lax.all_gather(small, "seq", axis=0)
    mod_size = mod_grad.size
    mod_all = small_all[:, :mod_size].reshape(images, 6, col_local)
    bias_sums = jnp.sum(small_all[:, mod_size:], axis=0)
    ada_bias_grad = jnp.sum(mod_all, axis=0)
    qv_bias_grad = bias_sums[: 2 * col_local].reshape(2, col_local)
    at = 2 * col_local
    proj_bias_grad = bias_sums[at : at + col_local]
    at += col_local
    hidden_bias_grad = bias_sums[at : at + hidden_bias.shape[0]]
    at += hidden_bias.shape[0]
    output_bias_grad = bias_sums[at:]
    width_start = seq_index * slice_width
    cond_cols = lax.dynamic_slice_in_dim(condition, width_start, slice_width, 1)
    low_cols = lax.dynamic_slice_in_dim(cond_low, width_start, slice_width, 1)
    ada_weight_grad = jnp.einsum(
        "wd,wcf->dcf", low_cols.astype(f32), mod_all, precision=HIGHEST, preferred_element_type=f32
    )
    ada_rows = lax.dynamic_slice_in_dim(ada_weight, width_start, slice_width, 0)
    cond_grad = lax.psum(
        jnp.einsum(
            "wcf,dcf->wd",
            mod_all,
            ada_rows.astype(f32),
            precision=HIGHEST,
            preferred_element_type=f32,
        ),
        "tp",
    )
    silu_pull = jax.vjp(jax.nn.silu, cond_cols)[1]
    class_grad = jnp.einsum(
        "wc,wd->cd",
        label_hot.astype(f32),
        silu_pull(cond_grad)[0],
        precision=HIGHEST,
        preferred_element_type=f32,
    )
    qkv_weight_grad, proj_weight_grad, hidden_weight_grad, output_weight_grad = (
        lax.psum_scatter(qkv_weight_term, "seq", scatter_dimension=0, tiled=True).astype(f32),
        lax.psum_scatter(proj_weight_term, "seq", scatter_dimension=1, tiled=True).astype(f32),
        lax.psum_scatter(hidden_weight_term, "seq", scatter_dimension=0, tiled=True).astype(f32),
        lax.psum_scatter(output_weight_term, "seq", scatter_dimension=1, tiled=True).astype(f32),
    )
    return (
        output,
        tokens_grad,
        class_grad,
        ada_weight_grad,
        ada_bias_grad,
        qkv_weight_grad,
        qv_bias_grad,
        proj_weight_grad,
        proj_bias_grad,
        hidden_weight_grad,
        hidden_bias_grad,
        output_weight_grad,
        output_bias_grad,
    )


def solution(mesh):
    return jax.shard_map(
        local,
        mesh=mesh,
        in_specs=(
            P("seq", "tp"),
            P("seq", "tp"),
            P("seq"),
            P(),
            P(),
            P(),
            P(),
            P(None, None, "tp"),
            P(None, "tp"),
            P(None, None, "tp"),
            P(None, "tp"),
            P("tp", None),
            P("tp"),
            P(None, "tp"),
            P("tp"),
            P("tp", None),
            P("tp"),
        ),
        out_specs=(
            P("seq", "tp"),
            P("seq", "tp"),
            P(None, "seq"),
            P("seq", None, "tp"),
            P(None, "tp"),
            P("seq", None, "tp"),
            P(None, "tp"),
            P("tp", "seq"),
            P("tp"),
            P("seq", "tp"),
            P("tp"),
            P("tp", "seq"),
            P("tp"),
        ),
        check_vma=False,
    )
```

profile of v0, /device:TPU:0, one launch (start us, length us, event | category | flops | bytes accessed | tf_op | source)
XLA Modules:
  0.0 589.2 jit_solution(4795627765267242598)
XLA Ops:
  9.4 2.4 fusion.24
  14.4 2.9 multiply_convert_fusion.4
  17.3 3.5 convolution_add_fusion.4
  21.1 26.5 %all_gather.22 = f32[4,6,1152]{1,0,2:T(4,128)S(1)} all-gather(f32[4,6,288]{1,0,2:T(4,128)S(1)} %copy.102), channel_id=1, replica_groups=mesh['seq'=8,'tp'=4] {'tp'}, dimensions={2}, use_global_device_ids=true | all-gather | bytes 138240 | tf_op jit(solution)/shard_map/all_gather | solution.py:102
  47.6 6.0 %fusion.109 = (f32[4,1,1152]{1,0,2:T(4,128)}, f32[4,1,1152]{1,0,2:T(4,128)}, f32[4,1,1152]{1,0,2:T(4,128)}, f32[4,1,1152]{1,0,2:T(4,128)}) fusion(f32[4,6,1152]{1,0,2:T(4,128)S(1)} %all_gather.22), kind=kLoop, calls=%fused_computation.184 | loop fusion | bytes 147456 | tf_op jit(solution)/shard_map/slice | solution.py:105
  53.6 2.1 copy.105
  55.7 2.3 copy.103
  59.4 3.1 fusion.59
  62.5 1.8 convert_reduce_fusion.1
  64.2 1.8 fusion.13
  66.1 3.9 fusion.21
  70.0 1.9 add_convert_fusion
  72.7 6.5 %fusion.113 = (f32[4,640]{1,0:T(4,128)S(1)}, f32[4,640,640]{1,2,0:T(8,128)}) fusion(pred[640,640]{0,1:T(8,128)(4,1)} %broadcast_compare_fusion, bf16[640,4,72]{0,2,1:T(8,128)(2,1)S(1)} %bitcast.99, bf16[640,4,72]{0,2,1:T(8,128)(2,1)S(1)} %bitcast.97), kind=kOutput, calls=%fused_computation.188 | convolution fusion | flops 242483840 | bytes 7710720 | tf_op jit(solution)/shard_map/sub | solution.py:150
  79.2 3.7 fusion.38
  83.7 2.2 convolution_convert_fusion.5
  85.9 2.7 convert_reduce_fusion.4
  88.8 25.1 %reduce-scatter.9.cloned.1.call-done = bf16[640,288]{0,1:T(8,128)(2,1)} async-done(((bf16[640,1152]{0,1:T(8,128)(2,1)}), bf16[640,288]{0,1:T(8,128)(2,1)}) %reduce-scatter.9.cloned.1.call-update) | async-done | bytes 368656 | tf_op jit(solution)/shard_map/reduce_scatter | solution.py:79
  113.9 2.9 fusion.78
  116.9 2.1 copy.111
  119.0 2.3 copy.109
  121.3 3.1 fusion.57
  124.4 10.8 %all-gather.10.cloned.1.call-done = bf16[640,1152]{0,1:T(8,128)(2,1)} async-done(((bf16[640,288]{0,1:T(8,128)(2,1)}), bf16[640,1152]{0,1:T(8,128)(2,1)}) %all-gather.10.cloned.1.call-update) | async-done | bytes 1474576 | tf_op jit(solution)/shard_map/all_gather | solution.py:76
  135.2 6.1 %fusion.115 = f32[640,1152]{0,1:T(8,128)} fusion(bf16[1152,1152]{1,0:T(8,128)(2,1)} %param.32, bf16[640,1152]{0,1:T(8,128)(2,1)} %all-gather.10.cloned.1.call-done), kind=kOutput, calls=%fused_computation.190 | convolution fusion | flops 1698693120 | bytes 7077888 | tf_op jit(solution)/shard_map/rd,fd->rf/dot_general | solution.py:180
  141.3 15.1 %all-gather.8.cloned.1.call-done = bf16[640,1152]{0,1:T(8,128)(2,1)} async-done(((bf16[640,288]{0,1:T(8,128)(2,1)}), bf16[640,1152]{0,1:T(8,128)(2,1)}) %all-gather.8.cloned.1.call-update) | async-done | bytes 1474576 | tf_op jit(solution)/shard_map/all_gather | solution.py:76
  156.4 1.8 convert_reduce_fusion
  158.2 1.8 fusion.12
  160.0 3.9 fusion.11
  164.0 6.0 %convert_reduce_fusion.2 = (f32[1152]{0:T(1024)S(1)}, bf16[640,1152]{0,1:T(8,128)(2,1)S(1)}, f32[640,1152]{0,1:T(8,128)}) fusion(f32[640,1152]{0,1:T(8,128)S(1)} %copy-done.43, f32[1152]{0:T(1024)S(1)} %convert_element_type.178, bf16[640,1152]{0,1:T(8,128)(2,1)S(1)} %fusion.11, bf16[1152,1152]{1,0:T(8,128)(2,1)S(1)} %copy-done), kind=kOutput, calls=%fused_computation.42 | convolution fusion | flops 1715649408 | bytes 11510784 | tf_op jit(solution)/shard_map/dot_general | solution.py:166
  171.2 4.0 convolution_convert_fusion.3
  175.2 3.4 fusion.4
  178.6 24.3 %reduce-scatter.13.cloned.1.call-done = bf16[640,288]{0,1:T(8,128)(2,1)} async-done(((bf16[640,1152]{0,1:T(8,128)(2,1)}), bf16[640,288]{0,1:T(8,128)(2,1)}) %reduce-scatter.13.cloned.1.call-update) | async-done | bytes 368656 | tf_op jit(solution)/shard_map/reduce_scatter | solution.py:79
  204.3 5.9 all-reduce.1
  210.2 2.9 convert_reduce_fusion.5
  213.2 6.6 %convolution_convert_fusion.4 = bf16[640,1152]{0,1:T(8,128)(2,1)} fusion(bf16[1152,1152]{1,0:T(8,128)(2,1)} %param.32, f32[640,1152]{0,1:T(8,128)} %get-tuple-element.54), kind=kOutput, calls=%fused_computation.28 | convolution fusion | flops 1706065920 | bytes 7077888 | tf_op jit(solution)/shard_map/dot_general | solution.py:171
  219.8 5.4 convolution_convert_fusion.1
  225.3 5.8 convolution_convert_fusion
  231.4 2.1 all-gather.12.cloned.1.call-done
  233.5 2.4 convolution_convert_fusion.7
  236.0 1.9 convolution_convert_fusion.6
  237.9 4.1 multiply_reduce_fusion
  244.0 2.0 fusion.37
  246.1 1.7 fusion.36
  247.9 4.3 fusion.41
  252.2 3.2 fusion.9
  255.8 1.9 fusion.2
  257.7 5.6 convolution_convert_fusion.2
  263.7 3.2 fusion.35
  267.2 71.5 %reduce-scatter.21.cloned.1.call-done = bf16[144,1152]{1,0:T(8,128)(2,1)} async-done(((bf16[1152,1152]{1,0:T(8,128)(2,1)}), bf16[144,1152]{1,0:T(8,128)(2,1)}) %reduce-scatter.21.cloned.1.call-update) | async-done | bytes 331792 | tf_op jit(solution)/shard_map/reduce_scatter | solution.py:293
  338.7 1.9 convert_element_type.205
  340.5 71.4 %reduce-scatter.23.cloned.1.call-done = bf16[1152,144]{0,1:T(8,128)(2,1)} async-done(((bf16[1152,1152]{0,1:T(8,128)(2,1)}), bf16[1152,144]{0,1:T(8,128)(2,1)}) %reduce-scatter.23.cloned.1.call-update) | async-done | bytes 331792 | tf_op jit(solution)/shard_map/reduce_scatter | solution.py:294
  412.0 1.9 convert_element_type.207
  413.8 62.3 %reduce-scatter.19.cloned.1.call-done = bf16[288,144]{0,1:T(8,128)(2,1)} async-done(((bf16[288,1152]{0,1:T(8,128)(2,1)}), bf16[288,144]{0,1:T(8,128)(2,1)}) %reduce-scatter.19.cloned.1.call-update) | async-done | bytes 82960 | tf_op jit(solution)/shard_map/reduce_scatter | solution.py:292
  476.1 1.6 convert_element_type.203
  477.7 27.7 %reduce-scatter.15.cloned.1.call-done = bf16[640,288]{0,1:T(8,128)(2,1)} async-done(((bf16[640,1152]{0,1:T(8,128)(2,1)}), bf16[640,288]{0,1:T(8,128)(2,1)}) %reduce-scatter.15.cloned.1.call-update) | async-done | bytes 368656 | tf_op jit(solution)/shard_map/reduce_scatter | solution.py:79
  506.4 1.6 fusion.75
  509.6 2.3 fusion.64
  512.1 31.6 %all-gather = f32[73728]{0:T(1024)S(1)} all-gather(f32[9216]{0:T(1024)S(1)} %concatenate.21), channel_id=2, replica_groups=mesh['seq'=8,'tp'=4] {'seq'}, dimensions={0}, use_global_device_ids=true | all-gather | bytes 331776 | tf_op jit(solution)/shard_map/all_gather | solution.py:253
  546.1 2.0 convolution_bitcast_fusion.1
  548.1 11.1 %all-reduce = (f32[640]{0:T(1024)S(1)}, f32[640]{0:T(1024)S(1)}, f32[32,144]{1,0:T(8,128)S(1)}) all-reduce(f32[640]{0:T(1024)S(1)} %broadcast_multiply_fusion, f32[640]{0:T(1024)S(1)} %broadcast_multiply_fusion.1, f32[32,144]{1,0:T(8,128)S(1)} %convolution_bitcast_fusion.1), channel_id=1, replica_groups=mesh['seq'=8,'tp'=4] {'tp'}, use_global_device_ids=true, to_apply=%region_22.23 | all-reduce | flops 5888 | bytes 47104 | tf_op jit(solution)/shard_map/psum | solution.py:114
  559.9 2.1 fusion.73
  562.0 1.8 fusion.61
  563.9 3.5 fusion.34
  567.3 12.9 %reduce-scatter.17.cloned.1.call-done = bf16[144,3,288]{2,0,1:T(8,128)(2,1)} async-done(((bf16[1152,3,288]{2,0,1:T(8,128)(2,1)}), bf16[144,3,288]{2,0,1:T(8,128)(2,1)}) %reduce-scatter.17.cloned.1.call-update) | async-done | bytes 248848 | tf_op jit(solution)/shard_map/reduce_scatter | solution.py:291
  580.2 1.9 convert_element_type.201
  (170 shorter events, 20.0 us)
Async XLA Ops:
  7.2 156.8 %copy-start = (bf16[1152,1152]{1,0:T(8,128)(2,1)S(1)}, bf16[1152,1152]{1,0:T(8,128)(2,1)}, u32[]{:S(2)}) copy-start(bf16[1152,1152]{1,0:T(8,128)(2,1)} %param.30) | copy-start | bytes 7962628
  7.2 55.3 %all-gather.6.cloned.1.call-start = ((), (), s32[]{:S(2)}) async-start(), calls=%async_computation.8 | async-start | bytes 1843200 | tf_op jit(solution)/shard_map/all_gather | solution.py:76
  9.3 4.4 copy-start.37
  9.3 4.7 copy-start.38
  9.3 4.7 copy-start.27
  9.3 5.1 copy-start.29
  11.8 1.1 copy-start.6
  13.7 100.2 %reduce-scatter.9.cloned.1.call-start = ((), (), s32[]{:S(2)}) async-start(), calls=%async_computation.9 | async-start | bytes 1843200 | tf_op jit(solution)/shard_map/reduce_scatter | solution.py:79
  53.6 4.6 copy-start.26
  62.5 3.6 copy-start.2
  66.1 3.9 copy-start.32
  70.0 1.9 copy-start.11
  72.7 6.5 %copy-start.16 = (bf16[640,1,288]{0,2,1:T(8,128)(2,1)}, bf16[640,1,288]{0,2,1:T(8,128)(2,1)S(1)}, u32[]{:S(2)}) copy-start(bf16[640,1,288]{0,2,1:T(8,128)(2,1)S(1)} %get-tuple-element.38) | copy-start | bytes 1105924
  72.7 6.5 %copy-start.17 = (bf16[640,1,288]{0,2,1:T(8,128)(2,1)}, bf16[640,1,288]{0,2,1:T(8,128)(2,1)S(1)}, u32[]{:S(2)}) copy-start(bf16[640,1,288]{0,2,1:T(8,128)(2,1)S(1)} %get-tuple-element.39) | copy-start | bytes 1105924
  79.2 4.5 copy-start.36
  82.9 0.7 copy-start.39
  83.7 5.1 copy-start.30
  85.9 31.0 %copy-start.28 = (bf16[1152]{0:T(1024)(128)(2,1)S(1)}, bf16[1152]{0:T(1024)(128)(2,1)}, u32[]{:S(2)}) copy-start(bf16[1152]{0:T(1024)(128)(2,1)} %param.31) | copy-start | bytes 6916
  85.9 49.3 %all-gather.10.cloned.1.call-start = ((), (), s32[]{:S(2)}) async-start(), calls=%async_computation.12 | async-start | bytes 1843200 | tf_op jit(solution)/shard_map/all_gather | solution.py:76
  88.7 67.7 %all-gather.8.cloned.1.call-start = ((), (), s32[]{:S(2)}) async-start(), calls=%async_computation.10 | async-start | bytes 1843200 | tf_op jit(solution)/shard_map/all_gather | solution.py:76
  116.8 86.1 %reduce-scatter.13.cloned.1.call-start = ((), (), s32[]{:S(2)}) async-start(), calls=%async_computation.13 | async-start | bytes 1843200 | tf_op jit(solution)/shard_map/reduce_scatter | solution.py:79
  156.4 3.6 copy-start.4
  160.0 4.0 copy-start.43
  164.0 6.0 %copy-start.12 = (bf16[640,1152]{0,1:T(8,128)(2,1)}, bf16[640,1152]{0,1:T(8,128)(2,1)S(1)}, u32[]{:S(2)}) copy-start(bf16[640,1152]{0,1:T(8,128)(2,1)S(1)} %fusion.11) | copy-start | bytes 4423684
  170.1 1.1 copy-start.44
  175.2 27.7 %copy-start.5 = (f32[640,1152]{0,1:T(8,128)S(1)}, f32[640,1152]{0,1:T(8,128)}, u32[]{:S(2)}) copy-start(f32[640,1152]{0,1:T(8,128)} %fusion.57) | copy-start | bytes 8847364
  175.2 58.3 %all-gather.12.cloned.1.call-start = ((), (), s32[]{:S(2)}) async-start(), calls=%async_computation.14 | async-start | bytes 1843200 | tf_op jit(solution)/shard_map/all_gather | solution.py:76
  213.1 50.6 %reduce-scatter.11.cloned.1.call-start = ((), (), s32[]{:S(2)}) async-start(), calls=%async_computation.11 | async-start | bytes 1843200 | tf_op jit(solution)/shard_map/reduce_scatter | solution.py:79
  213.2 6.7 %copy-start.13 = (bf16[640,1152]{0,1:T(8,128)(2,1)S(1)}, bf16[640,1152]{0,1:T(8,128)(2,1)}, u32[]{:S(2)}) copy-start(bf16[640,1152]{0,1:T(8,128)(2,1)} %copy-done.12) | copy-start | bytes 4423684
  219.8 5.6 copy-start.34
  219.8 118.9 %reduce-scatter.21.cloned.1.call-start = ((), (), s32[]{:S(2)}) async-start(), calls=%async_computation.18 | async-start | bytes 2985984 | tf_op jit(solution)/shard_map/reduce_scatter | solution.py:293
  225.3 186.7 %reduce-scatter.23.cloned.1.call-start = ((), (), s32[]{:S(2)}) async-start(), calls=%async_computation.19 | async-start | bytes 2985984 | tf_op jit(solution)/shard_map/reduce_scatter | solution.py:294
  231.2 4.7 copy-start.40
  231.2 244.9 %reduce-scatter.19.cloned.1.call-start = ((), (), s32[]{:S(2)}) async-start(), calls=%async_computation.17 | async-start | bytes 995328 | tf_op jit(solution)/shard_map/reduce_scatter | solution.py:292
  233.5 2.4 copy-start.35
  235.9 6.1 %copy-start.41 = (bf16[640,288]{0,1:T(8,128)(2,1)}, bf16[640,288]{0,1:T(8,128)(2,1)S(1)}, u32[]{:S(2)}) copy-start(bf16[640,288]{0,1:T(8,128)(2,1)S(1)} %convolution_convert_fusion.7) | copy-start | bytes 1105924
  235.9 1.9 copy-start.22
  237.9 4.3 slice-start
  237.9 5.1 slice-start.1
  243.0 1.0 copy-start.18
  246.0 259.4 %reduce-scatter.15.cloned.1.call-start = ((), (), s32[]{:S(2)}) async-start(), calls=%async_computation.15 | async-start | bytes 1843200 | tf_op jit(solution)/shard_map/reduce_scatter | solution.py:79
  246.1 1.7 copy-start.42
  247.8 4.4 copy-start.20
  247.8 4.4 copy-start.19
  247.8 4.4 copy-start.33
  252.2 3.3 copy-start.24
  252.2 3.5 copy-start.31
  252.2 3.5 copy-start.3
  255.4 2.2 copy-start.21
  255.5 324.8 %reduce-scatter.17.cloned.1.call-start = ((), (), s32[]{:S(2)}) async-start(), calls=%async_computation.16 | async-start | bytes 2985984 | tf_op jit(solution)/shard_map/reduce_scatter | solution.py:291
  257.7 6.0 %copy-start.7 = (f32[640,576]{0,1:T(8,128)S(1)}, f32[640,576]{0,1:T(8,128)}, u32[]{:S(2)}) copy-start(f32[640,576]{0,1:T(8,128)} %copy-done.6) | copy-start | bytes 4423684
  257.7 6.0 %copy-start.10 = (f32[640,288]{0,1:T(8,128)S(1)}, f32[640,288]{0,1:T(8,128)}, u32[]{:S(2)}) copy-start(f32[640,288]{0,1:T(8,128)} %get-tuple-element.52) | copy-start | bytes 2211844
  257.7 6.0 %copy-start.14 = (bf16[640,288]{0,1:T(8,128)(2,1)S(1)}, bf16[640,288]{0,1:T(8,128)(2,1)}, u32[]{:S(2)}) copy-start(bf16[640,288]{0,1:T(8,128)(2,1)} %reduce-scatter.9.cloned.1.call-done) | copy-start | bytes 1105924
  263.7 3.2 copy-start.25
  267.2 240.9 %copy-start.9 = (f32[640,288]{0,1:T(8,128)S(1)}, f32[640,288]{0,1:T(8,128)}, u32[]{:S(2)}) copy-start(f32[640,288]{0,1:T(8,128)} %get-tuple-element.30) | copy-start | bytes 2211844
  413.8 94.4 %copy-start.8 = (bf16[640,288]{0,1:T(8,128)(2,1)S(1)}, bf16[640,288]{0,1:T(8,128)(2,1)}, u32[]{:S(2)}) copy-start(bf16[640,288]{0,1:T(8,128)(2,1)} %reduce-scatter.13.cloned.1.call-done) | copy-start | bytes 1105924
  508.1 1.4 copy-start.23
  543.7 20.1 %copy-start.15 = (bf16[640,288]{0,1:T(8,128)(2,1)S(1)}, bf16[640,288]{0,1:T(8,128)(2,1)}, u32[]{:S(2)}) copy-start(bf16[640,288]{0,1:T(8,128)(2,1)} %reduce-scatter.15.cloned.1.call-done) | copy-start | bytes 1105924
  562.0 20.1 %copy-start.1 = (bf16[1152,1152]{1,0:T(8,128)(2,1)S(1)}, bf16[1152,1152]{1,0:T(8,128)(2,1)}, u32[]{:S(2)}) copy-start(bf16[1152,1152]{1,0:T(8,128)(2,1)} %param.30) | copy-start | bytes 7962628
Sparse Core Ops, SparseCore 0:
  13.8 29.6 all-gather.5
  86.0 27.8 reduce-scatter.8
  116.1 19.0 all-gather.9
  137.3 19.0 all-gather.7
  175.3 27.5 reduce-scatter.12
  213.2 20.2 all-gather.11
  236.1 27.5 reduce-scatter.10
  267.8 70.8 reduce-scatter.20
  342.4 69.5 reduce-scatter.22
  416.2 59.8 reduce-scatter.18
  478.9 26.4 reduce-scatter.14
  508.9 71.3 reduce-scatter.16
where the time goes:
time: 595 us; the launch traced here: 589 us
  waiting for transfers between devices  324 us (54%)
  matrix products  117 us (20%)
  blocking collectives  75 us (13%)
  other arithmetic  33.7 us (6%)
  local copies, waits for them, and re-layouts  23.8 us (4%)
  between operations  15.1 us (3%)
    reduce_scatter x4, waiting for transfers between devices, column_sum(): lax.psum_scatter(part_rows.astype(bf16), 'tp', scatter_dimension=1, tiled...  77.5 us
    reduce_scatter x1, waiting for transfers between devices, local(): lax.psum_scatter(hidden_weight_term, 'seq', scatter_dimension=0, tiled=True)  71.5 us
    reduce_scatter x1, waiting for transfers between devices, local(): lax.psum_scatter(output_weight_term, 'seq', scatter_dimension=1, tiled=True)  71.4 us
    reduce_scatter x1, waiting for transfers between devices, local(): lax.psum_scatter(proj_weight_term, 'seq', scatter_dimension=1, tiled=True)  62.3 us
    all_gather x1, blocking collectives, local(): small_all = lax.all_gather(small, 'seq', axis=0)  31.6 us
    all_gather x4, waiting for transfers between devices, whole_rows(): return lax.all_gather(part_rows, 'tp', axis=1, tiled=True)  28 us
    all_gather x1, blocking collectives, local(): mod_full = lax.all_gather(mod_own, 'tp', axis=2, tiled=True)  26.5 us
    dot_general x6, matrix products, exact_dot(): jnp.dot(left_mat, right_mat, precision=HIGHEST, preferred_element_type=jn...  19.7 us
  transfers between devices with their start and end apart: 12, of which 11 were waited for; matrix products, arithmetic and copies ran while one was open for 20% of the time, Pallas kernels for 0%

commit v1 on v0

--- a/solution.py
+++ b/solution.py
@@ -9,6 +9,18 @@
 ROWS = 640
 NORM_EPS = 1e-06
 HIGHEST = lax.Precision.HIGHEST
+
+
+def gather_by_bits(array, axis, dim):
+    ways, here, step = (lax.axis_size(axis), lax.axis_index(axis), array.shape[dim])
+    line, have = (array, 1)
+    while have < ways:
+        line = jnp.concatenate(
+            [line, lax.ppermute(line, axis, [(d, (d - have) % ways) for d in range(ways)])],
+            axis=dim,
+        )
+        have = 2 * have
+    return jnp.roll(line, here * step, axis=dim)
 
 
 def exact_dot(left_mat, right_mat):
@@ -99,7 +111,7 @@
         jnp.einsum("wd,dcf->wcf", cond_own, ada_weight, preferred_element_type=f32)
         + ada_bias.astype(f32)[None]
     )
-    mod_full = lax.all_gather(mod_own, "tp", axis=2, tiled=True)
+    mod_full = gather_by_bits(mod_own, "tp", 2)
 
     def row_full(stretch_id):
         return exact_dot(row_onehot, mod_full[:, stretch_id, :])

time: 595 us -> 569 us (0.956)
  blocking collectives: 75 us -> 48.6 us
  local copies, waits for them, and re-layouts: 23.8 us -> 8.91 us
  waiting for transfers between devices: 324 us -> 337 us
    all_gather x1 -> x0, blocking collectives: 26.5 us -> none  [local(): mod_full = lax.all_gather(mod_own, 'tp', axis=2, tiled=True)]
    slice x6 -> x1, local copies, waits for them, and re-layouts: 15 us -> 0.07 us  [the longest x5 14.9 us: row_full(): return exact_dot(row_onehot, mod_full[:, stretch_id, :])]
    ppermute x0 -> x2, waiting for transfers between devices: none -> 6.76 us  [gather_by_bits(): lax.ppermute(line, axis, [(d, (d - have) % ways) for d in range(ways)])]
  transfers between devices with their start and end apart: 12 -> 14, of which waited for: 11 -> 14; matrix products, arithmetic and copies ran while one was open for 20% -> 19% of each run, Pallas kernels for 0% -> 0%
where the time goes in v1:
time: 569 us; the launch traced here: 565 us
  waiting for transfers between devices  337 us (59%)
  matrix products  118 us (21%)
  blocking collectives  48.6 us (9%)
  other arithmetic  33.8 us (6%)
  between operations  15.1 us (3%)
  local copies, waits for them, and re-layouts  8.91 us (2%)
    reduce_scatter x4, waiting for transfers between devices, column_sum(): lax.psum_scatter(part_rows.astype(bf16), 'tp', scatter_dimension=1, tiled...  77.6 us
    reduce_scatter x1, waiting for transfers between devices, local(): lax.psum_scatter(output_weight_term, 'seq', scatter_dimension=1, tiled=True)  71.7 us
    reduce_scatter x1, waiting for transfers between devices, local(): lax.psum_scatter(hidden_weight_term, 'seq', scatter_dimension=0, tiled=True)  71.7 us
    reduce_scatter x1, waiting for transfers between devices, local(): lax.psum_scatter(proj_weight_term, 'seq', scatter_dimension=1, tiled=True)  62.5 us
    all_gather x4, waiting for transfers between devices, whole_rows(): return lax.all_gather(part_rows, 'tp', axis=1, tiled=True)  33.4 us
    all_gather x1, blocking collectives, local(): small_all = lax.all_gather(small, 'seq', axis=0)  31.7 us
    dot_general x6, matrix products, exact_dot(): jnp.dot(left_mat, right_mat, precision=HIGHEST, preferred_element_type=jn...  20.8 us
    psum x2, blocking collectives, input_grads(): lax.psum((jnp.sum(scaled_grad, axis=1, keepdims=True) / model_width, jnp....  16.8 us
  transfers between devices with their start and end apart: 14, of which 14 were waited for; matrix products, arithmetic and copies ran while one was open for 19% of the time, Pallas kernels for 0%

profile of v1, /device:TPU:0, one launch (start us, length us, event | category | flops | bytes accessed | tf_op | source)
XLA Modules:
  0.0 565.0 jit_solution(3516583838540602221)
XLA Ops:
  9.3 2.4 fusion.24
  14.2 2.9 multiply_convert_fusion.4
  17.1 3.5 convolution_add_fusion.4
  20.5 2.6 collective-permute-start
  25.5 6.1 %collective-permute-done.1 = f32[4,6,576]{2,0,1:T(4,128)S(1)} collective-permute-done((f32[4,6,576]{2,0,1:T(4,128)S(1)}, f32[4,6,576]{2,0,1:T(4,128)S(1)}, u32[]{:S(2)}, u32[]{:S(2)}) %collective-permute-start.1) | collective-permute-done | bytes 55328 | tf_op jit(solution)/shard_map/ppermute | solution.py:19
  31.9 3.2 fusion.59
  35.1 1.9 all-gather.6.cloned.1.call-done
  37.0 1.8 convert_reduce_fusion.1
  38.8 1.8 fusion.13
  40.6 4.0 fusion.21
  44.7 1.9 add_convert_fusion
  47.4 6.5 %fusion.112 = (f32[4,640]{1,0:T(4,128)S(1)}, f32[4,640,640]{1,2,0:T(8,128)}) fusion(pred[640,640]{0,1:T(8,128)(4,1)} %broadcast_compare_fusion, bf16[640,4,72]{0,2,1:T(8,128)(2,1)S(1)} %bitcast.99, bf16[640,4,72]{0,2,1:T(8,128)(2,1)S(1)} %bitcast.97), kind=kOutput, calls=%fused_computation.192 | convolution fusion | flops 242483840 | bytes 7710720 | tf_op jit(solution)/shard_map/sub | solution.py:162
  53.8 3.7 fusion.38
  58.3 2.2 convolution_convert_fusion.5
  60.6 2.7 convert_reduce_fusion.4
  63.4 25.2 %reduce-scatter.9.cloned.1.call-done = bf16[640,288]{0,1:T(8,128)(2,1)} async-done(((bf16[640,1152]{0,1:T(8,128)(2,1)}), bf16[640,288]{0,1:T(8,128)(2,1)}) %reduce-scatter.9.cloned.1.call-update) | async-done | bytes 368656 | tf_op jit(solution)/shard_map/reduce_scatter | solution.py:91
  88.6 2.9 fusion.78
  91.8 3.9 fusion.57
  95.7 14.3 %all-gather.10.cloned.1.call-done = bf16[640,1152]{0,1:T(8,128)(2,1)} async-done(((bf16[640,288]{0,1:T(8,128)(2,1)}), bf16[640,1152]{0,1:T(8,128)(2,1)}) %all-gather.10.cloned.1.call-update) | async-done | bytes 1474576 | tf_op jit(solution)/shard_map/all_gather | solution.py:88
  110.0 6.1 %fusion.114 = f32[640,1152]{0,1:T(8,128)} fusion(bf16[1152,1152]{1,0:T(8,128)(2,1)} %param.32, bf16[640,1152]{0,1:T(8,128)(2,1)} %all-gather.10.cloned.1.call-done), kind=kOutput, calls=%fused_computation.194 | convolution fusion | flops 1698693120 | bytes 7077888 | tf_op jit(solution)/shard_map/rd,fd->rf/dot_general | solution.py:192
  116.1 15.1 %all-gather.8.cloned.1.call-done = bf16[640,1152]{0,1:T(8,128)(2,1)} async-done(((bf16[640,288]{0,1:T(8,128)(2,1)}), bf16[640,1152]{0,1:T(8,128)(2,1)}) %all-gather.8.cloned.1.call-update) | async-done | bytes 1474576 | tf_op jit(solution)/shard_map/all_gather | solution.py:88
  131.2 1.8 convert_reduce_fusion
  133.0 1.8 fusion.12
  134.8 4.0 fusion.11
  138.9 6.0 %convert_reduce_fusion.2 = (f32[1152]{0:T(1024)S(1)}, bf16[640,1152]{0,1:T(8,128)(2,1)S(1)}, f32[640,1152]{0,1:T(8,128)}) fusion(f32[640,1152]{0,1:T(8,128)S(1)} %copy-done.44, f32[1152]{0:T(1024)S(1)} %convert_element_type.178, bf16[640,1152]{0,1:T(8,128)(2,1)S(1)} %fusion.11, bf16[1152,1152]{1,0:T(8,128)(2,1)S(1)} %copy-done), kind=kOutput, calls=%fused_computation.42 | convolution fusion | flops 1715649408 | bytes 11510784 | tf_op jit(solution)/shard_map/dot_general | solution.py:178
  144.9 1.1 copy-done.45
  146.1 3.9 convolution_convert_fusion.3
  150.1 3.4 fusion.4
  153.5 24.3 %reduce-scatter.13.cloned.1.call-done = bf16[640,288]{0,1:T(8,128)(2,1)} async-done(((bf16[640,1152]{0,1:T(8,128)(2,1)}), bf16[640,288]{0,1:T(8,128)(2,1)}) %reduce-scatter.13.cloned.1.call-update) | async-done | bytes 368656 | tf_op jit(solution)/shard_map/reduce_scatter | solution.py:91
  177.7 1.4 fusion.74
  179.1 5.9 %all-reduce.1 = (f32[640]{0:T(1024)S(1)}, f32[640]{0:T(1024)S(1)}) all-reduce(f32[640]{0:T(1024)S(1)} %get-tuple-element.53, f32[640]{0:T(1024)S(1)} %get-tuple-element.54), channel_id=1, replica_groups=mesh['seq'=8,'tp'=4] {'tp'}, use_global_device_ids=true, to_apply=%region_16.17 | all-reduce | flops 1280 | bytes 10240 | tf_op jit(solution)/shard_map/psum | solution.py:126
  185.0 2.9 convert_reduce_fusion.5
  188.0 6.5 %convolution_convert_fusion.4 = bf16[640,1152]{0,1:T(8,128)(2,1)} fusion(bf16[1152,1152]{1,0:T(8,128)(2,1)} %param.32, f32[640,1152]{0,1:T(8,128)} %get-tuple-element.50), kind=kOutput, calls=%fused_computation.28 | convolution fusion | flops 1706065920 | bytes 7077888 | tf_op jit(solution)/shard_map/dot_general | solution.py:183
  194.6 5.4 convolution_convert_fusion.1
  200.2 5.8 %convolution_convert_fusion = bf16[1152,1152]{0,1:T(8,128)(2,1)} fusion(bf16[640,1152]{0,1:T(8,128)(2,1)S(1)} %copy-done.35, f32[640,1152]{0,1:T(8,128)} %get-tuple-element.50), kind=kOutput, calls=%fused_computation.1 | convolution fusion | flops 1706655744 | bytes 7077888 | tf_op jit(solution)/shard_map/rf,rd->fd/dot_general | solution.py:189
  206.2 2.1 all-gather.12.cloned.1.call-done
  208.4 2.4 convolution_convert_fusion.7
  210.8 1.9 convolution_convert_fusion.6
  212.7 4.1 multiply_reduce_fusion
  218.8 2.0 fusion.37
  220.9 1.7 fusion.36
  222.7 4.3 fusion.41
  227.1 3.2 fusion.9
  230.6 1.9 fusion.2
  232.5 5.5 convolution_convert_fusion.2
  238.5 3.2 fusion.35
  242.0 71.7 %reduce-scatter.21.cloned.1.call-done = bf16[144,1152]{1,0:T(8,128)(2,1)} async-done(((bf16[1152,1152]{1,0:T(8,128)(2,1)}), bf16[144,1152]{1,0:T(8,128)(2,1)}) %reduce-scatter.21.cloned.1.call-update) | async-done | bytes 331792 | tf_op jit(solution)/shard_map/reduce_scatter | solution.py:305
  313.7 1.9 convert_element_type.205
  315.5 71.7 %reduce-scatter.23.cloned.1.call-done = bf16[1152,144]{0,1:T(8,128)(2,1)} async-done(((bf16[1152,1152]{0,1:T(8,128)(2,1)}), bf16[1152,144]{0,1:T(8,128)(2,1)}) %reduce-scatter.23.cloned.1.call-update) | async-done | bytes 331792 | tf_op jit(solution)/shard_map/reduce_scatter | solution.py:306
  387.2 1.9 convert_element_type.207
  389.1 62.5 %reduce-scatter.19.cloned.1.call-done = bf16[288,144]{0,1:T(8,128)(2,1)} async-done(((bf16[288,1152]{0,1:T(8,128)(2,1)}), bf16[288,144]{0,1:T(8,128)(2,1)}) %reduce-scatter.19.cloned.1.call-update) | async-done | bytes 82960 | tf_op jit(solution)/shard_map/reduce_scatter | solution.py:304
  451.6 1.6 convert_element_type.203
  453.2 27.7 %reduce-scatter.15.cloned.1.call-done = bf16[640,288]{0,1:T(8,128)(2,1)} async-done(((bf16[640,1152]{0,1:T(8,128)(2,1)}), bf16[640,288]{0,1:T(8,128)(2,1)}) %reduce-scatter.15.cloned.1.call-update) | async-done | bytes 368656 | tf_op jit(solution)/shard_map/reduce_scatter | solution.py:91
  481.9 1.6 fusion.75
  483.7 1.2 fusion.48
  485.1 2.3 fusion.64
  487.6 31.7 %all-gather = f32[73728]{0:T(1024)S(1)} all-gather(f32[9216]{0:T(1024)S(1)} %concatenate.33), channel_id=2, replica_groups=mesh['seq'=8,'tp'=4] {'seq'}, dimensions={0}, use_global_device_ids=true | all-gather | bytes 331776 | tf_op jit(solution)/shard_map/all_gather | solution.py:265
  521.6 2.0 convolution_bitcast_fusion.1
  523.7 11.0 %all-reduce = (f32[640]{0:T(1024)S(1)}, f32[640]{0:T(1024)S(1)}, f32[32,144]{1,0:T(8,128)S(1)}) all-reduce(f32[640]{0:T(1024)S(1)} %broadcast_multiply_fusion, f32[640]{0:T(1024)S(1)} %broadcast_multiply_fusion.1, f32[32,144]{1,0:T(8,128)S(1)} %convolution_bitcast_fusion.1), channel_id=1, replica_groups=mesh['seq'=8,'tp'=4] {'tp'}, use_global_device_ids=true, to_apply=%region_22.23 | all-reduce | flops 5888 | bytes 47104 | tf_op jit(solution)/shard_map/psum | solution.py:126
  535.3 2.1 fusion.73
  537.5 1.8 fusion.61
  539.3 3.5 fusion.34
  542.8 13.2 %reduce-scatter.17.cloned.1.call-done = bf16[144,3,288]{2,0,1:T(8,128)(2,1)} async-done(((bf16[1152,3,288]{2,0,1:T(8,128)(2,1)}), bf16[144,3,288]{2,0,1:T(8,128)(2,1)}) %reduce-scatter.17.cloned.1.call-update) | async-done | bytes 248848 | tf_op jit(solution)/shard_map/reduce_scatter | solution.py:303
  556.0 1.9 convert_element_type.201
  (171 shorter events, 17.4 us)
Async XLA Ops:
  7.2 131.7 %copy-start = (bf16[1152,1152]{1,0:T(8,128)(2,1)S(1)}, bf16[1152,1152]{1,0:T(8,128)(2,1)}, u32[]{:S(2)}) copy-start(bf16[1152,1152]{1,0:T(8,128)(2,1)} %param.30) | copy-start | bytes 7962628
  7.2 29.8 %all-gather.6.cloned.1.call-start = ((), (), s32[]{:S(2)}) async-start(), calls=%async_computation.8 | async-start | bytes 1843200 | tf_op jit(solution)/shard_map/all_gather | solution.py:88
  9.3 4.4 copy-start.38
  9.3 4.4 copy-start.28
  9.3 4.8 copy-start.30
  11.8 1.1 copy-start.6
  13.7 74.9 %reduce-scatter.9.cloned.1.call-start = ((), (), s32[]{:S(2)}) async-start(), calls=%async_computation.9 | async-start | bytes 1843200 | tf_op jit(solution)/shard_map/reduce_scatter | solution.py:91
  14.2 8.9 %copy-start.39 = (s32[32]{0:T(128)S(1)}, s32[32]{0:T(128)}, u32[]{:S(2)}) copy-start(s32[32]{0:T(128)} %param.20) | copy-start | bytes 388
  14.2 10.3 %copy-start.27 = (bf16[2,288]{1,0:T(2,128)(2,1)S(1)}, bf16[2,288]{1,0:T(2,128)(2,1)}, u32[]{:S(2)}) copy-start(bf16[2,288]{1,0:T(2,128)(2,1)} %param.27) | copy-start | bytes 3460
  20.5 4.7 collective-permute-start
  25.4 6.2 %collective-permute-start.1 = (f32[4,6,576]{2,0,1:T(4,128)S(1)}, f32[4,6,576]{2,0,1:T(4,128)S(1)}, u32[]{:S(2)}, u32[]{:S(2)}) collective-permute-start(f32[4,6,576]{2,0,1:T(4,128)S(1)} %pad_maximum_fusion.1), channel_id=1, source_target_pairs={{0,2},{1,3},{2,0},{3,1},{4,6},{5,7},{6,4},{7,5},{8,10},{9,11},{10,... | collective-permute-start | bytes 165896 | tf_op jit(solution)/shard_map/ppermute | solution.py:19
  31.8 8.7 %copy-start.22 = (f32[4,6,2304]{2,0,1:T(4,128)}, f32[4,6,2304]{2,0,1:T(4,128)S(1)}, u32[]{:S(2)}) copy-start(f32[4,6,2304]{2,0,1:T(4,128)S(1)} %concatenate.31) | copy-start | bytes 663556
  37.0 3.6 copy-start.2
  40.6 4.0 copy-start.33
  44.6 1.9 copy-start.11
  47.4 6.5 %copy-start.16 = (bf16[640,1,288]{0,2,1:T(8,128)(2,1)}, bf16[640,1,288]{0,2,1:T(8,128)(2,1)S(1)}, u32[]{:S(2)}) copy-start(bf16[640,1,288]{0,2,1:T(8,128)(2,1)S(1)} %get-tuple-element.34) | copy-start | bytes 1105924
  47.4 6.5 %copy-start.17 = (bf16[640,1,288]{0,2,1:T(8,128)(2,1)}, bf16[640,1,288]{0,2,1:T(8,128)(2,1)S(1)}, u32[]{:S(2)}) copy-start(bf16[640,1,288]{0,2,1:T(8,128)(2,1)S(1)} %get-tuple-element.35) | copy-start | bytes 1105924
  53.8 4.5 copy-start.37
  57.6 0.7 copy-start.40
  58.3 5.1 copy-start.31
  60.5 31.3 %copy-start.29 = (bf16[1152]{0:T(1024)(128)(2,1)S(1)}, bf16[1152]{0:T(1024)(128)(2,1)}, u32[]{:S(2)}) copy-start(bf16[1152]{0:T(1024)(128)(2,1)} %param.31) | copy-start | bytes 6916
  60.5 49.4 %all-gather.10.cloned.1.call-start = ((), (), s32[]{:S(2)}) async-start(), calls=%async_computation.12 | async-start | bytes 1843200 | tf_op jit(solution)/shard_map/all_gather | solution.py:88
  63.3 67.9 %all-gather.8.cloned.1.call-start = ((), (), s32[]{:S(2)}) async-start(), calls=%async_computation.10 | async-start | bytes 1843200 | tf_op jit(solution)/shard_map/all_gather | solution.py:88
  91.6 86.2 %reduce-scatter.13.cloned.1.call-start = ((), (), s32[]{:S(2)}) async-start(), calls=%async_computation.13 | async-start | bytes 1843200 | tf_op jit(solution)/shard_map/reduce_scatter | solution.py:91
  131.2 3.6 copy-start.4
  134.8 4.1 copy-start.44
  138.9 6.1 %copy-start.12 = (bf16[640,1152]{0,1:T(8,128)(2,1)}, bf16[640,1152]{0,1:T(8,128)(2,1)S(1)}, u32[]{:S(2)}) copy-start(bf16[640,1152]{0,1:T(8,128)(2,1)S(1)} %fusion.11) | copy-start | bytes 4423684
  144.9 1.1 copy-start.45
  150.0 27.7 %copy-start.5 = (f32[640,1152]{0,1:T(8,128)S(1)}, f32[640,1152]{0,1:T(8,128)}, u32[]{:S(2)}) copy-start(f32[640,1152]{0,1:T(8,128)} %fusion.57) | copy-start | bytes 8847364
  150.0 58.3 %all-gather.12.cloned.1.call-start = ((), (), s32[]{:S(2)}) async-start(), calls=%async_computation.14 | async-start | bytes 1843200 | tf_op jit(solution)/shard_map/all_gather | solution.py:88
  188.0 50.5 %reduce-scatter.11.cloned.1.call-start = ((), (), s32[]{:S(2)}) async-start(), calls=%async_computation.11 | async-start | bytes 1843200 | tf_op jit(solution)/shard_map/reduce_scatter | solution.py:91
  188.0 6.6 %copy-start.13 = (bf16[640,1152]{0,1:T(8,128)(2,1)S(1)}, bf16[640,1152]{0,1:T(8,128)(2,1)}, u32[]{:S(2)}) copy-start(bf16[640,1152]{0,1:T(8,128)(2,1)} %copy-done.12) | copy-start | bytes 4423684
  194.6 5.6 copy-start.35
  194.6 119.1 %reduce-scatter.21.cloned.1.call-start = ((), (), s32[]{:S(2)}) async-start(), calls=%async_computation.18 | async-start | bytes 2985984 | tf_op jit(solution)/shard_map/reduce_scatter | solution.py:305
  200.1 187.1 %reduce-scatter.23.cloned.1.call-start = ((), (), s32[]{:S(2)}) async-start(), calls=%async_computation.19 | async-start | bytes 2985984 | tf_op jit(solution)/shard_map/reduce_scatter | solution.py:306
  206.0 4.8 copy-start.41
  206.0 245.6 %reduce-scatter.19.cloned.1.call-start = ((), (), s32[]{:S(2)}) async-start(), calls=%async_computation.17 | async-start | bytes 995328 | tf_op jit(solution)/shard_map/reduce_scatter | solution.py:304
  208.4 2.4 copy-start.36
  210.8 6.1 %copy-start.42 = (bf16[640,288]{0,1:T(8,128)(2,1)}, bf16[640,288]{0,1:T(8,128)(2,1)S(1)}, u32[]{:S(2)}) copy-start(bf16[640,288]{0,1:T(8,128)(2,1)S(1)} %convolution_convert_fusion.7) | copy-start | bytes 1105924
  210.8 1.9 copy-start.23
  212.7 4.3 slice-start
  212.7 5.1 slice-start.1
  217.8 1.0 copy-start.18
  220.9 260.0 %reduce-scatter.15.cloned.1.call-start = ((), (), s32[]{:S(2)}) async-start(), calls=%async_computation.15 | async-start | bytes 1843200 | tf_op jit(solution)/shard_map/reduce_scatter | solution.py:91
  220.9 1.7 copy-start.43
  222.7 4.4 copy-start.20
  222.7 4.4 copy-start.19
  222.7 4.4 copy-start.34
  227.0 3.3 copy-start.25
  227.1 3.5 copy-start.32
  227.1 3.5 copy-start.3
  230.3 2.2 copy-start.21
  230.3 325.7 %reduce-scatter.17.cloned.1.call-start = ((), (), s32[]{:S(2)}) async-start(), calls=%async_computation.16 | async-start | bytes 2985984 | tf_op jit(solution)/shard_map/reduce_scatter | solution.py:303
  232.5 6.0 %copy-start.7 = (f32[640,576]{0,1:T(8,128)S(1)}, f32[640,576]{0,1:T(8,128)}, u32[]{:S(2)}) copy-start(f32[640,576]{0,1:T(8,128)} %copy-done.6) | copy-start | bytes 4423684
  232.5 6.0 %copy-start.10 = (f32[640,288]{0,1:T(8,128)S(1)}, f32[640,288]{0,1:T(8,128)}, u32[]{:S(2)}) copy-start(f32[640,288]{0,1:T(8,128)} %get-tuple-element.48) | copy-start | bytes 2211844
  232.5 6.0 %copy-start.14 = (bf16[640,288]{0,1:T(8,128)(2,1)S(1)}, bf16[640,288]{0,1:T(8,128)(2,1)}, u32[]{:S(2)}) copy-start(bf16[640,288]{0,1:T(8,128)(2,1)} %reduce-scatter.9.cloned.1.call-done) | copy-start | bytes 1105924
  238.5 3.2 copy-start.26
  242.0 241.6 %copy-start.9 = (f32[640,288]{0,1:T(8,128)S(1)}, f32[640,288]{0,1:T(8,128)}, u32[]{:S(2)}) copy-start(f32[640,288]{0,1:T(8,128)} %get-tuple-element.30) | copy-start | bytes 2211844
  389.1 94.6 %copy-start.8 = (bf16[640,288]{0,1:T(8,128)(2,1)S(1)}, bf16[640,288]{0,1:T(8,128)(2,1)}, u32[]{:S(2)}) copy-start(bf16[640,288]{0,1:T(8,128)(2,1)} %reduce-scatter.13.cloned.1.call-done) | copy-start | bytes 1105924
  483.5 1.4 copy-start.24
  519.3 20.0 %copy-start.15 = (bf16[640,288]{0,1:T(8,128)(2,1)S(1)}, bf16[640,288]{0,1:T(8,128)(2,1)}, u32[]{:S(2)}) copy-start(bf16[640,288]{0,1:T(8,128)(2,1)} %reduce-scatter.15.cloned.1.call-done) | copy-start | bytes 1105924
  537.5 20.4 %copy-start.1 = (bf16[1152,1152]{1,0:T(8,128)(2,1)S(1)}, bf16[1152,1152]{1,0:T(8,128)(2,1)}, u32[]{:S(2)}) copy-start(bf16[1152,1152]{1,0:T(8,128)(2,1)} %param.30) | copy-start | bytes 7962628
Sparse Core Ops, SparseCore 0:
  13.8 23.1 all-gather.5
  60.7 27.9 reduce-scatter.8
  90.8 19.0 all-gather.9
  112.0 19.0 all-gather.7
  150.2 27.5 reduce-scatter.12
  188.1 20.2 all-gather.11
  210.9 27.5 reduce-scatter.10
  242.6 71.0 reduce-scatter.20
  317.3 69.8 reduce-scatter.22
  391.4 60.0 reduce-scatter.18
  454.3 26.4 reduce-scatter.14
  484.3 71.6 reduce-scatter.16
